TPU v7x, 256 devices: a whole 4x4x8 slice. The times are simulated.
256 devices in a mesh: seq: 32 (over x_hi, z, core), tp: 8 (over y, x_lo).
Axes of the slice: x: 4 (x_hi: 2, x_lo: 2; x = x_hi * 2 + x_lo), y: 4, z: 8, core: 2. Of those that a mesh axis runs over, the one named last changes fastest.
Arguments:
- queries: bfloat16 [8, 4096, 4096], P('tp', 'seq'), may hold values from -9 to 9
- key_rows: bfloat16 [8, 4096, 4096], P('tp', 'seq'), may hold values from -6 to 6
- values: bfloat16 [8, 4096, 4096], P('tp', 'seq'), may hold values from -6 to 6
- upstream: bfloat16 [8, 4096, 4096], P(None, 'seq', 'tp'), may hold values from -6 to 6
- out_weight: bfloat16 [4096, 4096], P(None, 'tp'), may hold values from -0.09375 to 0.09375
- blocks: int32 [64, 4], replicated, may hold values from 0 to 63, as said below
Outputs:
- attended: bfloat16 [8, 4096, 4096], P('tp', 'seq')
- grad_queries: bfloat16 [8, 4096, 4096], P('tp', 'seq')
- grad_keys: bfloat16 [8, 4096, 4096], P('tp', 'seq')
- grad_values: bfloat16 [8, 4096, 4096], P('tp', 'seq')
- grad_weight: float32 [4096, 4096], P('seq', 'tp')
Inputs may be any that keep to these rules, and one draw needn't show every extreme that they name: Row a lists the blocks a - 1, a and a + 1 modulo 64, then one block 2 to 62 blocks after a modulo 64; no row names a block twice.
All inputs are finite; a program needn't handle non-finite values.
Results may differ from a plain program's by a relative error of at most 0.022.
Values may be sent and summed in bfloat16 or wider, within the bound.
A program may use at most 128 MiB of HBM per device.

v0:
```python
import math
import jax
import jax.numpy as jnp
from jax import lax
from jax.sharding import PartitionSpec as P

HD = 128
BLK = 64
NB = 4


def forward_head(query_rows, key_rows, value_rows, blocks):
    block_count = blocks.shape[0]
    factor = 1.0 / math.sqrt(HD)
    query_tiles = query_rows.reshape(block_count, BLK, HD)
    key_set = key_rows.reshape(block_count, BLK, HD)[blocks].reshape(block_count, NB * BLK, HD)
    value_set = value_rows.reshape(block_count, BLK, HD)[blocks].reshape(block_count, NB * BLK, HD)
    scores = (
        jnp.einsum("qid,qjd->qij", query_tiles, key_set, preferred_element_type=jnp.float32)
        * factor
    )
    row_max = jnp.max(scores, axis=-1, keepdims=True)
    shifted = jnp.exp(scores - row_max)
    soft_probs = shifted / jnp.sum(shifted, axis=-1, keepdims=True)
    probs_low = soft_probs.astype(jnp.bfloat16)
    context = jnp.einsum(
        "qij,qjd->qid", probs_low, value_set, preferred_element_type=jnp.float32
    ).astype(jnp.bfloat16)
    return (context, soft_probs, probs_low, key_set, value_set)


def backward_head(query_rows, grad_rows, blocks, saved):
    context, soft_probs, probs_low, key_set, value_set = saved
    block_count = blocks.shape[0]
    factor = 1.0 / math.sqrt(HD)
    query_tiles = query_rows.reshape(block_count, BLK, HD)
    grad_tiles = grad_rows.reshape(block_count, BLK, HD)
    row_delta = jnp.sum(
        grad_tiles.astype(jnp.float32) * context.astype(jnp.float32), axis=-1, keepdims=True
    )
    dprobs = jnp.einsum("qid,qjd->qij", grad_tiles, value_set, preferred_element_type=jnp.float32)
    dscores = (soft_probs * (dprobs - row_delta) * factor).astype(jnp.bfloat16)
    query_grad = jnp.einsum(
        "qij,qjd->qid", dscores, key_set, preferred_element_type=jnp.float32
    ).astype(jnp.bfloat16)
    flat_list = blocks.reshape(-1)
    key_parts = jnp.einsum(
        "qij,qid->qjd", dscores, query_tiles, preferred_element_type=jnp.float32
    ).reshape(block_count * NB, BLK, HD)
    value_parts = jnp.einsum(
        "qij,qid->qjd", probs_low, grad_tiles, preferred_element_type=jnp.float32
    ).reshape(block_count * NB, BLK, HD)
    key_grad = (
        jnp.zeros((block_count, BLK, HD), jnp.float32)
        .at[flat_list]
        .add(key_parts)
        .astype(jnp.bfloat16)
    )
    value_grad = (
        jnp.zeros((block_count, BLK, HD), jnp.float32)
        .at[flat_list]
        .add(value_parts)
        .astype(jnp.bfloat16)
    )
    return (query_grad, key_grad, value_grad)


def on_device(queries, key_rows, values, upstream, out_weight, blocks):
    head_queries, head_keys, head_values = (
        lax.all_to_all(queries, "seq", split_axis=2, concat_axis=1, tiled=True),
        lax.all_to_all(key_rows, "seq", split_axis=2, concat_axis=1, tiled=True),
        lax.all_to_all(values, "seq", split_axis=2, concat_axis=1, tiled=True),
    )
    length = head_queries.shape[1]
    count_heads = head_queries.shape[2] // HD

    def split_heads(array):
        return array.reshape(length, count_heads, HD).transpose(1, 0, 2)

    def join_heads(array):
        return (
            array.reshape(count_heads, length, HD)
            .transpose(1, 0, 2)
            .reshape(1, length, count_heads * HD)
        )

    grad_tokens = lax.psum_scatter(
        jnp.einsum("stc,dc->std", upstream, out_weight, preferred_element_type=jnp.float32).astype(
            jnp.bfloat16
        ),
        "tp",
        scatter_dimension=0,
        tiled=True,
    )
    grad_heads = lax.all_to_all(grad_tokens, "seq", split_axis=2, concat_axis=1, tiled=True)
    stacked = (
        split_heads(head_queries),
        split_heads(head_keys),
        split_heads(head_values),
        split_heads(grad_heads),
    )

    def both_one(packed):
        saved_one = forward_head(packed[0], packed[1], packed[2], blocks)
        return (saved_one[0],) + backward_head(packed[0], packed[3], blocks, saved_one)

    results = lax.map(both_one, stacked)
    attended, query_grad, key_grad, value_grad = (
        lax.all_to_all(join_heads(results[0]), "seq", split_axis=1, concat_axis=2, tiled=True),
        lax.all_to_all(join_heads(results[1]), "seq", split_axis=1, concat_axis=2, tiled=True),
        lax.all_to_all(join_heads(results[2]), "seq", split_axis=1, concat_axis=2, tiled=True),
        lax.all_to_all(join_heads(results[3]), "seq", split_axis=1, concat_axis=2, tiled=True),
    )
    every_sequence = lax.all_gather(attended, "tp", axis=0, tiled=True)
    grad_weight = lax.psum_scatter(
        jnp.einsum(
            "str,stc->rc", every_sequence, upstream, preferred_element_type=jnp.float32
        ).astype(jnp.bfloat16),
        "seq",
        scatter_dimension=0,
        tiled=True,
    ).astype(jnp.float32)
    return (attended, query_grad, key_grad, value_grad, grad_weight)


def solution(mesh):
    in_specs = (
        P("tp", "seq", None),
        P("tp", "seq", None),
        P("tp", "seq", None),
        P(None, "seq", "tp"),
        P(None, "tp"),
        P(),
    )
    out_specs = (
        P("tp", "seq", None),
        P("tp", "seq", None),
        P("tp", "seq", None),
        P("tp", "seq", None),
        P("seq", "tp"),
    )
    return jax.shard_map(
        on_device, mesh=mesh, in_specs=in_specs, out_specs=out_specs, check_vma=False
    )
```

profile of v0, /device:TPU:32, one launch (start us, length us, event | category | flops | bytes accessed | tf_op | source)
XLA Modules:
  0.0 871.2 jit_solution(8195947875667358401)
XLA Ops:
  8.4 8.9 %convolution_convert_fusion = bf16[8,128,4096]{2,1,0:T(8,128)(2,1)} fusion(bf16[8,128,512]{2,1,0:T(8,128)(2,1)S(1)} %copy-done, bf16[4096,512]{1,0:T(8,128)(2,1)} %param.10), kind=kOutput, calls=%fused_computation.6 | convolution fusion | flops 4299161600 | bytes 13631488 | tf_op jit(solution)/shard_map/stc,dc->std/dot_general | solution.py:88
  17.3 5.0 copy.81
  22.9 23.4 %reduce.1 = bf16[4096,128]{1,0:T(8,128)(2,1)} reduce(bf16[4096,1,128]{2,1,0:T(2,128)(2,1)S(1)} %bitcast.130, bf16[]{:T(256)} %broadcast.81), dimensions={1}, to_apply=%bitcast.71.reduce_sub_computation | reduce | bytes 2097154
  46.3 2.1 reshape.139
  48.4 11.9 %all-to-all-start.2 = ((bf16[32,2,8192]{2,1,0:T(2,128)(2,1)}), bf16[32,2,8192]{2,1,0:T(2,128)(2,1)}, u32[]{:S(2)}, u32[]{:S(2)}) async-start(bf16[32,2,8192]{2,1,0:T(2,128)(2,1)} %reshape.139), calls=%async_computation.2 | async-start | bytes 2097152 | tf_op jit(solution)/shard_map/all_to_all | solution.py:72
  60.3 5.0 copy.76
  65.3 23.4 %reduce.2 = bf16[4096,128]{1,0:T(8,128)(2,1)} reduce(bf16[4096,1,128]{2,1,0:T(2,128)(2,1)S(1)} %bitcast.136, bf16[]{:T(256)} %broadcast.81), dimensions={1}, to_apply=%bitcast.73.reduce_sub_computation | reduce | bytes 2097154
  88.7 2.1 reshape.141
  90.8 9.9 %all-to-all-start = ((bf16[32,2,8192]{2,1,0:T(2,128)(2,1)}), bf16[32,2,8192]{2,1,0:T(2,128)(2,1)}, u32[]{:S(2)}, u32[]{:S(2)}) async-start(bf16[32,2,8192]{2,1,0:T(2,128)(2,1)} %reshape.141), calls=%async_computation | async-start | bytes 2097152 | tf_op jit(solution)/shard_map/all_to_all | solution.py:71
  100.7 5.0 copy.79
  105.8 23.4 %reduce.3 = bf16[4096,128]{1,0:T(8,128)(2,1)} reduce(bf16[4096,1,128]{2,1,0:T(2,128)(2,1)S(1)} %bitcast.137, bf16[]{:T(256)} %broadcast.81), dimensions={1}, to_apply=%bitcast.75.reduce_sub_computation | reduce | bytes 2097154
  129.1 2.1 reshape.143
  131.4 10.1 %all-to-all-start.1 = ((bf16[32,2,8192]{2,1,0:T(2,128)(2,1)}), bf16[32,2,8192]{2,1,0:T(2,128)(2,1)}, u32[]{:S(2)}, u32[]{:S(2)}) async-start(bf16[32,2,8192]{2,1,0:T(2,128)(2,1)} %reshape.143), calls=%async_computation.1 | async-start | bytes 2097152 | tf_op jit(solution)/shard_map/all_to_all | solution.py:70
  141.5 84.0 %reduce-scatter.3.cloned.1.call-done = bf16[1,128,4096]{2,1,0:T(8,128)(2,1)} async-done(((bf16[8,128,4096]{2,1,0:T(8,128)(2,1)}), bf16[1,128,4096]{2,1,0:T(8,128)(2,1)}) %reduce-scatter.3.cloned.1.call-update) | async-done | bytes 1048592 | tf_op jit(solution)/shard_map/reduce_scatter | solution.py:87
  225.5 5.0 copy.85
  230.6 23.4 %reduce = bf16[4096,128]{1,0:T(8,128)(2,1)} reduce(bf16[4096,1,128]{2,1,0:T(2,128)(2,1)S(1)} %bitcast.132, bf16[]{:T(256)} %broadcast.81), dimensions={1}, to_apply=%bitcast.79.reduce_sub_computation | reduce | bytes 2097154
  253.9 2.1 reshape.147
  256.1 9.8 %all-to-all-start.4 = ((bf16[32,2,8192]{2,1,0:T(2,128)(2,1)}), bf16[32,2,8192]{2,1,0:T(2,128)(2,1)}, u32[]{:S(2)}, u32[]{:S(2)}) async-start(bf16[32,2,8192]{2,1,0:T(2,128)(2,1)} %reshape.147), calls=%async_computation.5 | async-start | bytes 2097152 | tf_op jit(solution)/shard_map/all_to_all | solution.py:95
  266.2 4.3 reshape.140
  271.6 1.6 copy.82
  273.2 5.8 reshape.142
  279.0 2.7 copy.101
  281.7 1.6 copy.77
  283.3 3.0 gather_fusion.1
  286.3 3.0 gather_fusion
  289.4 4.3 reshape.144
  294.8 1.6 copy.80
  296.4 3.8 fusion.24
  300.2 2.0 copy-done.2
  302.2 2.9 fusion.21
  305.0 5.8 reshape.148
  310.8 1.7 copy.105
  312.5 1.3 copy.86
  313.9 12.7 %multiply_reduce_fusion = (f32[64,64]{1,0:T(8,128)S(1)}, bf16[64,64,128]{2,1,0:T(8,128)(2,1)S(1)}) fusion(bf16[64,64,128]{2,1,0:T(8,128)(2,1)} %bitcast.156, bf16[64,256,128]{2,1,0:T(8,128)(2,1)} %bitcast.149, f32[64,64]{1,0:T(8,128)S(1)} %get-tuple-element.65, f32[64,256,64]{1,2,0:T(8,128)} %copy-done.2), kind=kOutput, calls=%fused_computation.14 | convolution fusion | flops 276300032 | bytes 10518528 | tf_op jit(solution)/shard_map/while/body/eval_jaxpr/qij,qjd->qid/dot_general | solution.py:26
  326.6 17.5 %copy.116 = bf16[1,4096,128]{2,0,1:T(2,128)(2,1)} copy(bf16[1,4096,128]{2,1,0:T(8,128)(2,1)S(1)} %bitcast.155) | data formatting | bytes 2097152 | tf_op jit(solution)/shard_map/reshape;transpose;reshape | solution.py:84
  344.0 23.4 %reduce.4 = bf16[4096,128]{1,0:T(8,128)(2,1)S(1)} reduce(bf16[4096,1,128]{2,1,0:T(2,128)(2,1)} %bitcast.133, bf16[]{:T(256)} %broadcast.81), dimensions={1}, to_apply=%bitcast.113.reduce_sub_computation | reduce | bytes 2097154
  368.6 40.3 %all_to_all.132 = bf16[32,2,8192]{2,1,0:T(2,128)(2,1)S(1)} all-to-all(bf16[32,2,8192]{2,1,0:T(2,128)(2,1)} %reshape.145), channel_id=1, replica_groups=mesh['seq'=32,'tp'=8] {'seq'}, dimensions={0} | all-to-all | bytes 2097152 | tf_op jit(solution)/shard_map/all_to_all | solution.py:109
  408.9 3.5 reshape.146
  412.3 1.7 copy.104
  415.4 2.3 copy.96
  417.7 7.5 multiply_convert_fusion
  425.2 158.5 %all-gather.2.cloned.1.call-done = bf16[8,128,4096]{2,1,0:T(8,128)(2,1)} async-done(((bf16[1,128,4096]{2,1,0:T(8,128)(2,1)}), bf16[8,128,4096]{2,1,0:T(8,128)(2,1)}) %all-gather.2.cloned.1.call-update) | async-done | bytes 8388624 | tf_op jit(solution)/shard_map/all_gather | solution.py:114
  583.7 9.7 %bitcast_convert_fusion = bf16[4096,512]{1,0:T(8,128)(2,1)} fusion(bf16[8,128,4096]{2,1,0:T(8,128)(2,1)} %all-gather.2.cloned.1.call-done, bf16[8,128,512]{2,1,0:T(8,128)(2,1)S(1)} %copy-done), kind=kOutput, calls=%fused_computation.5 | convolution fusion | flops 4297064448 | bytes 13631488 | tf_op jit(solution)/shard_map/str,stc->rc/dot_general | solution.py:116
  593.5 3.7 convolution_convert_fusion.1
  597.2 17.0 %copy.115 = bf16[1,4096,128]{2,0,1:T(2,128)(2,1)} copy(bf16[1,4096,128]{2,1,0:T(8,128)(2,1)S(1)} %bitcast.138) | data formatting | bytes 2097152 | tf_op jit(solution)/shard_map/reshape;transpose;reshape | solution.py:84
  614.2 23.5 %reduce.5 = bf16[4096,128]{1,0:T(8,128)(2,1)S(1)} reduce(bf16[4096,1,128]{2,1,0:T(2,128)(2,1)} %bitcast.134, bf16[]{:T(256)} %broadcast.81), dimensions={1}, to_apply=%bitcast.112.reduce_sub_computation | reduce | bytes 2097154
  638.8 10.2 %all-to-all-start.5 = ((bf16[32,2,8192]{2,1,0:T(2,128)(2,1)}), bf16[32,2,8192]{2,1,0:T(2,128)(2,1)}, u32[]{:S(2)}, u32[]{:S(2)}) async-start(bf16[32,2,8192]{2,1,0:T(2,128)(2,1)} %reshape.149), calls=%async_computation.6 | async-start | bytes 2097152 | tf_op jit(solution)/shard_map/all_to_all | solution.py:110
  649.2 6.1 fusion.25
  655.5 26.3 %scatter_fusion = f32[64,64,128]{2,1,0:T(8,128)S(1)} fusion(f32[64,64,128]{2,1,0:T(8,128)S(1)} %broadcast.50.clone, s32[256]{0:T(256)S(1)} %bitcast.159, f32[256,64,128]{2,1,0:T(8,128)} %bitcast.116), kind=kCustom, calls=%fused_computation.2 | custom fusion | flops 2097152 | bytes 25166848 | tf_op jit(solution)/shard_map/while/body/eval_jaxpr/scatter-add | solution.py:56
  682.0 16.7 %copy.114 = bf16[1,4096,128]{2,0,1:T(2,128)(2,1)S(1)} copy(bf16[1,4096,128]{2,1,0:T(8,128)(2,1)S(1)} %bitcast.139) | data formatting | bytes 2097152 | tf_op jit(solution)/shard_map/reshape;transpose;reshape | solution.py:84
  698.8 22.4 %reduce.6 = bf16[4096,128]{1,0:T(8,128)(2,1)S(1)} reduce(bf16[4096,1,128]{2,1,0:T(2,128)(2,1)S(1)} %bitcast.135, bf16[]{:T(256)} %broadcast.81), dimensions={1}, to_apply=%bitcast.111.reduce_sub_computation | reduce | bytes 2097154
  722.3 10.3 %all-to-all-start.6 = ((bf16[32,2,8192]{2,1,0:T(2,128)(2,1)}), bf16[32,2,8192]{2,1,0:T(2,128)(2,1)}, u32[]{:S(2)}, u32[]{:S(2)}) async-start(bf16[32,2,8192]{2,1,0:T(2,128)(2,1)} %reshape.151), calls=%async_computation.7 | async-start | bytes 2097152 | tf_op jit(solution)/shard_map/all_to_all | solution.py:111
  732.6 14.2 %fusion.10 = f32[64,256,128]{2,1,0:T(8,128)} fusion(bf16[64,64,128]{2,1,0:T(8,128)(2,1)S(1)} %bitcast.158, f32[64,64]{1,0:T(8,128)S(1)} %get-tuple-element.65, f32[64,256,64]{1,2,0:T(8,128)} %copy-done.2), kind=kOutput, calls=%fused_computation.24 | convolution fusion | flops 273682688 | bytes 13647872 | tf_op jit(solution)/shard_map/while/body/eval_jaxpr/qij,qid->qjd/dot_general | solution.py:50
  747.0 26.2 %scatter_fusion.1 = f32[64,64,128]{2,1,0:T(8,128)S(1)} fusion(f32[64,64,128]{2,1,0:T(8,128)S(1)} %broadcast.50.clone.1, s32[256]{0:T(256)S(1)} %bitcast.160, f32[256,64,128]{2,1,0:T(8,128)} %bitcast.129), kind=kCustom, calls=%fused_computation.3 | custom fusion | flops 2097152 | bytes 25166848 | tf_op jit(solution)/shard_map/while/body/eval_jaxpr/scatter-add | solution.py:62
  773.5 16.7 %copy.113 = bf16[1,4096,128]{2,0,1:T(2,128)(2,1)S(1)} copy(bf16[1,4096,128]{2,1,0:T(8,128)(2,1)S(1)} %bitcast.140) | data formatting | bytes 2097152 | tf_op jit(solution)/shard_map/reshape;transpose;reshape | solution.py:84
  790.2 22.4 %reduce.7 = bf16[4096,128]{1,0:T(8,128)(2,1)S(1)} reduce(bf16[4096,1,128]{2,1,0:T(2,128)(2,1)S(1)} %bitcast.131, bf16[]{:T(256)} %broadcast.81), dimensions={1}, to_apply=%bitcast.110.reduce_sub_computation | reduce | bytes 2097154
  813.7 9.9 %all-to-all-start.7 = ((bf16[32,2,8192]{2,1,0:T(2,128)(2,1)}), bf16[32,2,8192]{2,1,0:T(2,128)(2,1)}, u32[]{:S(2)}, u32[]{:S(2)}) async-start(bf16[32,2,8192]{2,1,0:T(2,128)(2,1)} %reshape.153), calls=%async_computation.8 | async-start | bytes 2097152 | tf_op jit(solution)/shard_map/all_to_all | solution.py:112
  823.6 4.3 reshape.150
  828.7 1.3 copy.97
  830.0 4.3 reshape.152
  836.5 17.7 %all-to-all-done.7 = bf16[32,2,8192]{2,1,0:T(2,128)(2,1)} async-done(((bf16[32,2,8192]{2,1,0:T(2,128)(2,1)}), bf16[32,2,8192]{2,1,0:T(2,128)(2,1)}, u32[]{:S(2)}, u32[]{:S(2)}) %all-to-all-start.7) | async-done | bytes 1048608 | tf_op jit(solution)/shard_map/all_to_all | solution.py:112
  854.1 4.4 reshape.154
  859.6 1.6 copy.93
  862.6 1.6 convert_element_type.51
  (48 shorter events, 16.6 us)
Async XLA Ops:
  7.2 1.2 copy-start
  7.2 218.3 %reduce-scatter.3.cloned.1.call-start = ((), (), s32[]{:S(2)}) async-start(), calls=%async_computation.10 | async-start | bytes 9437184 | tf_op jit(solution)/shard_map/reduce_scatter | solution.py:87
  48.4 42.4 %all-to-all-start.2 = ((bf16[32,2,8192]{2,1,0:T(2,128)(2,1)}), bf16[32,2,8192]{2,1,0:T(2,128)(2,1)}, u32[]{:S(2)}, u32[]{:S(2)}) async-start(bf16[32,2,8192]{2,1,0:T(2,128)(2,1)} %reshape.139), calls=%async_computation.2 | async-start | bytes 2097152 | tf_op jit(solution)/shard_map/all_to_all | solution.py:72
  90.8 40.5 %all-to-all-start = ((bf16[32,2,8192]{2,1,0:T(2,128)(2,1)}), bf16[32,2,8192]{2,1,0:T(2,128)(2,1)}, u32[]{:S(2)}, u32[]{:S(2)}) async-start(bf16[32,2,8192]{2,1,0:T(2,128)(2,1)} %reshape.141), calls=%async_computation | async-start | bytes 2097152 | tf_op jit(solution)/shard_map/all_to_all | solution.py:71
  131.4 124.7 %all-to-all-start.1 = ((bf16[32,2,8192]{2,1,0:T(2,128)(2,1)}), bf16[32,2,8192]{2,1,0:T(2,128)(2,1)}, u32[]{:S(2)}, u32[]{:S(2)}) async-start(bf16[32,2,8192]{2,1,0:T(2,128)(2,1)} %reshape.143), calls=%async_computation.1 | async-start | bytes 2097152 | tf_op jit(solution)/shard_map/all_to_all | solution.py:70
  230.5 35.4 %copy-start.4 = (s32[64,4]{0,1:T(4,128)S(1)}, s32[64,4]{0,1:T(4,128)}, u32[]{:S(2)}) copy-start(s32[64,4]{0,1:T(4,128)} %param.11) | copy-start | bytes 3076
  256.1 49.0 %all-to-all-start.4 = ((bf16[32,2,8192]{2,1,0:T(2,128)(2,1)}), bf16[32,2,8192]{2,1,0:T(2,128)(2,1)}, u32[]{:S(2)}, u32[]{:S(2)}) async-start(bf16[32,2,8192]{2,1,0:T(2,128)(2,1)} %reshape.147), calls=%async_computation.5 | async-start | bytes 2097152 | tf_op jit(solution)/shard_map/all_to_all | solution.py:95
  265.9 317.8 %all-gather.2.cloned.1.call-start = ((), (), s32[]{:S(2)}) async-start(), calls=%async_computation.11 | async-start | bytes 9437184 | tf_op jit(solution)/shard_map/all_gather | solution.py:114
  300.2 2.0 copy-start.2
  417.7 444.9 %reduce-scatter.5.cloned.1.call-start = ((), (), s32[]{:S(2)}) async-start(), calls=%async_computation.12 | async-start | bytes 4325376 | tf_op jit(solution)/shard_map/reduce_scatter | solution.py:115
  638.8 83.5 %all-to-all-start.5 = ((bf16[32,2,8192]{2,1,0:T(2,128)(2,1)}), bf16[32,2,8192]{2,1,0:T(2,128)(2,1)}, u32[]{:S(2)}, u32[]{:S(2)}) async-start(bf16[32,2,8192]{2,1,0:T(2,128)(2,1)} %reshape.149), calls=%async_computation.6 | async-start | bytes 2097152 | tf_op jit(solution)/shard_map/all_to_all | solution.py:110
  721.2 11.4 %copy-start.3 = (bf16[1,32,128,128]{3,2,1,0:T(8,128)(2,1)S(1)}, bf16[1,32,128,128]{3,2,1,0:T(8,128)(2,1)}, u32[]{:S(2)}) copy-start(bf16[1,32,128,128]{3,2,1,0:T(8,128)(2,1)} %copy.86) | copy-start | bytes 3145732
  722.3 91.4 %all-to-all-start.6 = ((bf16[32,2,8192]{2,1,0:T(2,128)(2,1)}), bf16[32,2,8192]{2,1,0:T(2,128)(2,1)}, u32[]{:S(2)}, u32[]{:S(2)}) async-start(bf16[32,2,8192]{2,1,0:T(2,128)(2,1)} %reshape.151), calls=%async_computation.7 | async-start | bytes 2097152 | tf_op jit(solution)/shard_map/all_to_all | solution.py:111
  813.7 40.4 %all-to-all-start.7 = ((bf16[32,2,8192]{2,1,0:T(2,128)(2,1)}), bf16[32,2,8192]{2,1,0:T(2,128)(2,1)}, u32[]{:S(2)}, u32[]{:S(2)}) async-start(bf16[32,2,8192]{2,1,0:T(2,128)(2,1)} %reshape.153), calls=%async_computation.8 | async-start | bytes 2097152 | tf_op jit(solution)/shard_map/all_to_all | solution.py:112
  854.1 10.1 %copy-start.1 = (bf16[8,128,512]{2,1,0:T(8,128)(2,1)S(1)}, bf16[8,128,512]{2,1,0:T(8,128)(2,1)}, u32[]{:S(2)}) copy-start(bf16[8,128,512]{2,1,0:T(8,128)(2,1)} %param.9) | copy-start | bytes 3145732
Sparse Core Ops, SparseCore 0:
  17.5 208.0 reduce-scatter.2
  417.8 165.8 all-gather.1
  593.6 137.1 reduce-scatter.4
where the time goes:
time: 881 us; the launch traced here: 871 us
  waiting for transfers between devices  260 us (30%)
  other arithmetic  243 us (28%)
  local copies, waits for them, and re-layouts  175 us (20%)
  starting transfers between devices  72.2 us (8%)
  matrix products  66.5 us (8%)
  blocking collectives  40.3 us (5%)
  between operations  14.6 us (2%)
    unnamed x8, other arithmetic  185 us
    all_gather x1, waiting for transfers between devices, on_device(): every_sequence = lax.all_gather(attended, 'tp', axis=0, tiled=True)  159 us
    unnamed x43, local copies, waits for them, and re-layouts  84.4 us
    reduce_scatter x1, waiting for transfers between devices, on_device(): lax.psum_scatter(jnp.einsum('stc,dc->std', upstream, out_weight, preferre...  84 us
    another operation x4, local copies, waits for them, and re-layouts, join_heads(): return array.reshape(count_heads, length, HD).transpose(1, 0, 2).reshape(...  68 us
    all_to_all x1, blocking collectives, on_device(): lax.all_to_all(join_heads(results[0]), 'seq', split_axis=1, concat_axis=2...  40.3 us
    scatter-add x1, other arithmetic, backward_head(): key_grad = jnp.zeros((block_count, BLK, HD), jnp.float32).at[flat_list].a...  26.3 us
    scatter-add x1, other arithmetic, backward_head(): value_grad = jnp.zeros((block_count, BLK, HD), jnp.float32).at[flat_list]...  26.2 us
  transfers between devices with their start and end apart: 10, of which 4 were waited for; matrix products, arithmetic and copies ran while one was open for 45% of the time, Pallas kernels for 0%

commit v1 on v0

--- a/solution.py
+++ b/solution.py
@@ -106,7 +106,15 @@
 
     results = lax.map(both_one, stacked)
     attended, query_grad, key_grad, value_grad = (
-        lax.all_to_all(join_heads(results[0]), "seq", split_axis=1, concat_axis=2, tiled=True),
+        jnp.concatenate(
+            lax.all_to_all(
+                jnp.stack(jnp.split(join_heads(results[0]), lax.axis_size("seq"), axis=1)),
+                "seq",
+                0,
+                0,
+            ),
+            axis=2,
+        ),
         lax.all_to_all(join_heads(results[1]), "seq", split_axis=1, concat_axis=2, tiled=True),
         lax.all_to_all(join_heads(results[2]), "seq", split_axis=1, concat_axis=2, tiled=True),
         lax.all_to_all(join_heads(results[3]), "seq", split_axis=1, concat_axis=2, tiled=True),

time: 881 us -> 832 us (0.944)
  local copies, waits for them, and re-layouts: 175 us -> 149 us
  other arithmetic: 243 us -> 219 us
    unnamed x8 -> x7, other arithmetic: 185 us -> 162 us
    another operation x4 -> x3, local copies, waits for them, and re-layouts: 68 us -> 50.5 us  [join_heads(): return array.reshape(count_heads, length, HD).transpose(1, 0, 2).reshape(...]
    unnamed x43 -> x72, local copies, waits for them, and re-layouts: 84.4 us -> 76.2 us
  transfers between devices with their start and end apart: 10 -> 10, of which waited for: 4 -> 4; matrix products, arithmetic and copies ran while one was open for 45% -> 47% of each run, Pallas kernels for 0% -> 0%
where the time goes in v1:
time: 832 us; the launch traced here: 822 us
  waiting for transfers between devices  261 us (31%)
  other arithmetic  219 us (26%)
  local copies, waits for them, and re-layouts  149 us (18%)
  starting transfers between devices  72.1 us (9%)
  matrix products  66.2 us (8%)
  blocking collectives  40.4 us (5%)
  between operations  14.7 us (2%)
    unnamed x7, other arithmetic  162 us
    all_gather x1, waiting for transfers between devices, on_device(): every_sequence = lax.all_gather(attended, 'tp', axis=0, tiled=True)  159 us
    reduce_scatter x1, waiting for transfers between devices, on_device(): lax.psum_scatter(jnp.einsum('stc,dc->std', upstream, out_weight, preferre...  84.1 us
    unnamed x72, local copies, waits for them, and re-layouts  76.2 us
    another operation x3, local copies, waits for them, and re-layouts, join_heads(): return array.reshape(count_heads, length, HD).transpose(1, 0, 2).reshape(...  50.5 us
    all_to_all x1, blocking collectives, on_device(): lax.all_to_all(jnp.stack(jnp.split(join_heads(results[0]), lax.axis_size(...  40.4 us
    scatter-add x1, other arithmetic, backward_head(): key_grad = jnp.zeros((block_count, BLK, HD), jnp.float32).at[flat_list].a...  26.3 us
    scatter-add x1, other arithmetic, backward_head(): value_grad = jnp.zeros((block_count, BLK, HD), jnp.float32).at[flat_list]...  26.2 us
  transfers between devices with their start and end apart: 10, of which 4 were waited for; matrix products, arithmetic and copies ran while one was open for 47% of the time, Pallas kernels for 0%

profile of v1, /device:TPU:32, one launch (start us, length us, event | category | flops | bytes accessed | tf_op | source)
XLA Modules:
  0.0 822.1 jit_solution(14633177357248879832)
XLA Ops:
  7.2 1.2 copy-done
  8.4 8.9 %convolution_convert_fusion = bf16[8,128,4096]{2,1,0:T(8,128)(2,1)} fusion(bf16[8,128,512]{2,1,0:T(8,128)(2,1)S(1)} %copy-done, bf16[4096,512]{1,0:T(8,128)(2,1)} %param.10), kind=kOutput, calls=%fused_computation.6 | convolution fusion | flops 4299161600 | bytes 13631488 | tf_op jit(solution)/shard_map/stc,dc->std/dot_general | solution.py:88
  17.3 5.0 copy.80
  22.9 23.4 %reduce.1 = bf16[4096,128]{1,0:T(8,128)(2,1)} reduce(bf16[4096,1,128]{2,1,0:T(2,128)(2,1)S(1)} %bitcast.255, bf16[]{:T(256)} %broadcast.81), dimensions={1}, to_apply=%bitcast.199.reduce_sub_computation | reduce | bytes 2097154
  46.3 2.1 reshape.147
  48.4 11.6 %all-to-all-start.2 = ((bf16[32,2,8192]{2,1,0:T(2,128)(2,1)}), bf16[32,2,8192]{2,1,0:T(2,128)(2,1)}, u32[]{:S(2)}, u32[]{:S(2)}) async-start(bf16[32,2,8192]{2,1,0:T(2,128)(2,1)} %reshape.147), calls=%async_computation.2 | async-start | bytes 2097152 | tf_op jit(solution)/shard_map/all_to_all | solution.py:72
  60.0 5.0 copy.75
  65.1 23.4 %reduce.2 = bf16[4096,128]{1,0:T(8,128)(2,1)} reduce(bf16[4096,1,128]{2,1,0:T(2,128)(2,1)S(1)} %bitcast.260, bf16[]{:T(256)} %broadcast.81), dimensions={1}, to_apply=%bitcast.201.reduce_sub_computation | reduce | bytes 2097154
  88.4 2.1 reshape.149
  90.6 9.9 %all-to-all-start = ((bf16[32,2,8192]{2,1,0:T(2,128)(2,1)}), bf16[32,2,8192]{2,1,0:T(2,128)(2,1)}, u32[]{:S(2)}, u32[]{:S(2)}) async-start(bf16[32,2,8192]{2,1,0:T(2,128)(2,1)} %reshape.149), calls=%async_computation | async-start | bytes 2097152 | tf_op jit(solution)/shard_map/all_to_all | solution.py:71
  100.4 5.0 copy.78
  105.5 23.4 %reduce.3 = bf16[4096,128]{1,0:T(8,128)(2,1)} reduce(bf16[4096,1,128]{2,1,0:T(2,128)(2,1)S(1)} %bitcast.261, bf16[]{:T(256)} %broadcast.81), dimensions={1}, to_apply=%bitcast.203.reduce_sub_computation | reduce | bytes 2097154
  128.9 2.1 reshape.151
  131.1 10.3 %all-to-all-start.1 = ((bf16[32,2,8192]{2,1,0:T(2,128)(2,1)}), bf16[32,2,8192]{2,1,0:T(2,128)(2,1)}, u32[]{:S(2)}, u32[]{:S(2)}) async-start(bf16[32,2,8192]{2,1,0:T(2,128)(2,1)} %reshape.151), calls=%async_computation.1 | async-start | bytes 2097152 | tf_op jit(solution)/shard_map/all_to_all | solution.py:70
  141.5 84.1 %reduce-scatter.3.cloned.1.call-done = bf16[1,128,4096]{2,1,0:T(8,128)(2,1)} async-done(((bf16[8,128,4096]{2,1,0:T(8,128)(2,1)}), bf16[1,128,4096]{2,1,0:T(8,128)(2,1)}) %reduce-scatter.3.cloned.1.call-update) | async-done | bytes 1048592 | tf_op jit(solution)/shard_map/reduce_scatter | solution.py:87
  225.5 5.0 copy.83
  230.6 23.4 %reduce = bf16[4096,128]{1,0:T(8,128)(2,1)} reduce(bf16[4096,1,128]{2,1,0:T(2,128)(2,1)S(1)} %bitcast.257, bf16[]{:T(256)} %broadcast.81), dimensions={1}, to_apply=%bitcast.205.reduce_sub_computation | reduce | bytes 2097154
  253.9 2.1 reshape.153
  256.1 9.8 %all-to-all-start.4 = ((bf16[32,2,8192]{2,1,0:T(2,128)(2,1)}), bf16[32,2,8192]{2,1,0:T(2,128)(2,1)}, u32[]{:S(2)}, u32[]{:S(2)}) async-start(bf16[32,2,8192]{2,1,0:T(2,128)(2,1)} %reshape.153), calls=%async_computation.5 | async-start | bytes 2097152 | tf_op jit(solution)/shard_map/all_to_all | solution.py:95
  266.1 4.3 reshape.148
  270.5 1.1 copy.99
  271.6 1.6 copy.81
  273.2 5.8 reshape.150
  279.0 2.7 copy.97
  281.7 1.6 copy.76
  283.3 3.1 gather_fusion.1
  286.3 3.0 gather_fusion
  289.4 4.3 reshape.152
  294.8 1.6 copy.79
  296.4 3.8 fusion.24
  300.2 2.0 copy-done.2
  302.1 2.9 fusion.21
  305.0 5.8 reshape.154
  310.8 1.7 copy.100
  312.5 1.3 copy.84
  313.8 12.7 %multiply_reduce_fusion = (f32[64,64]{1,0:T(8,128)S(1)}, bf16[64,64,128]{2,1,0:T(8,128)(2,1)S(1)}) fusion(bf16[64,64,128]{2,1,0:T(8,128)(2,1)} %bitcast.309, bf16[64,256,128]{2,1,0:T(8,128)(2,1)} %bitcast.272, f32[64,64]{1,0:T(8,128)S(1)} %get-tuple-element.65, f32[64,256,64]{1,2,0:T(8,128)} %copy-done.2), kind=kOutput, calls=%fused_computation.14 | convolution fusion | flops 276300032 | bytes 10518528 | tf_op jit(solution)/shard_map/while/body/eval_jaxpr/qij,qjd->qid/dot_general | solution.py:26
  327.0 40.4 %all_to_all.119 = bf16[32,1,128,128]{3,2,1,0:T(8,128)(2,1)S(1)} all-to-all(bf16[32,1,128,128]{3,2,1,0:T(8,128)(2,1)S(1)} %constant_dynamic-update-slice_fusion), channel_id=1, replica_groups=mesh['seq'=32,'tp'=8] {'seq'}, dimensions={0} | all-to-all | bytes 2097152 | tf_op jit(solution)/shard_map/all_to_all | solution.py:110
  367.4 1.1 copy_bitcast_fusion
  368.6 7.1 multiply_convert_fusion
  375.7 158.9 %all-gather.2.cloned.1.call-done = bf16[8,128,4096]{2,1,0:T(8,128)(2,1)} async-done(((bf16[1,128,4096]{2,1,0:T(8,128)(2,1)}), bf16[8,128,4096]{2,1,0:T(8,128)(2,1)}) %all-gather.2.cloned.1.call-update) | async-done | bytes 8388624 | tf_op jit(solution)/shard_map/all_gather | solution.py:122
  534.6 9.7 %bitcast_convert_fusion = bf16[4096,512]{1,0:T(8,128)(2,1)} fusion(bf16[8,128,4096]{2,1,0:T(8,128)(2,1)} %all-gather.2.cloned.1.call-done, bf16[8,128,512]{2,1,0:T(8,128)(2,1)S(1)} %copy-done), kind=kOutput, calls=%fused_computation.5 | convolution fusion | flops 4297064448 | bytes 13631488 | tf_op jit(solution)/shard_map/str,stc->rc/dot_general | solution.py:124
  544.4 3.7 convolution_convert_fusion.1
  548.1 17.1 %copy.111 = bf16[1,4096,128]{2,0,1:T(2,128)(2,1)} copy(bf16[1,4096,128]{2,1,0:T(8,128)(2,1)S(1)} %bitcast.262) | data formatting | bytes 2097152 | tf_op jit(solution)/shard_map/reshape;transpose;reshape | solution.py:84
  565.2 23.5 %reduce.4 = bf16[4096,128]{1,0:T(8,128)(2,1)S(1)} reduce(bf16[4096,1,128]{2,1,0:T(2,128)(2,1)} %bitcast.258, bf16[]{:T(256)} %broadcast.81), dimensions={1}, to_apply=%bitcast.239.reduce_sub_computation | reduce | bytes 2097154
  589.7 10.2 %all-to-all-start.5 = ((bf16[32,2,8192]{2,1,0:T(2,128)(2,1)}), bf16[32,2,8192]{2,1,0:T(2,128)(2,1)}, u32[]{:S(2)}, u32[]{:S(2)}) async-start(bf16[32,2,8192]{2,1,0:T(2,128)(2,1)} %reshape.155), calls=%async_computation.6 | async-start | bytes 2097152 | tf_op jit(solution)/shard_map/all_to_all | solution.py:118
  600.1 6.1 fusion.25
  606.5 26.3 %scatter_fusion = f32[64,64,128]{2,1,0:T(8,128)S(1)} fusion(f32[64,64,128]{2,1,0:T(8,128)S(1)} %broadcast.50.clone, s32[256]{0:T(256)S(1)} %bitcast.312, f32[256,64,128]{2,1,0:T(8,128)} %bitcast.242), kind=kCustom, calls=%fused_computation.2 | custom fusion | flops 2097152 | bytes 25166848 | tf_op jit(solution)/shard_map/while/body/eval_jaxpr/scatter-add | solution.py:56
  633.0 16.7 %copy.110 = bf16[1,4096,128]{2,0,1:T(2,128)(2,1)S(1)} copy(bf16[1,4096,128]{2,1,0:T(8,128)(2,1)S(1)} %bitcast.263) | data formatting | bytes 2097152 | tf_op jit(solution)/shard_map/reshape;transpose;reshape | solution.py:84
  649.7 22.4 %reduce.5 = bf16[4096,128]{1,0:T(8,128)(2,1)S(1)} reduce(bf16[4096,1,128]{2,1,0:T(2,128)(2,1)S(1)} %bitcast.259, bf16[]{:T(256)} %broadcast.81), dimensions={1}, to_apply=%bitcast.238.reduce_sub_computation | reduce | bytes 2097154
  673.2 10.3 %all-to-all-start.6 = ((bf16[32,2,8192]{2,1,0:T(2,128)(2,1)}), bf16[32,2,8192]{2,1,0:T(2,128)(2,1)}, u32[]{:S(2)}, u32[]{:S(2)}) async-start(bf16[32,2,8192]{2,1,0:T(2,128)(2,1)} %reshape.157), calls=%async_computation.7 | async-start | bytes 2097152 | tf_op jit(solution)/shard_map/all_to_all | solution.py:119
  683.6 14.2 %fusion.10 = f32[64,256,128]{2,1,0:T(8,128)} fusion(bf16[64,64,128]{2,1,0:T(8,128)(2,1)S(1)} %bitcast.311, f32[64,64]{1,0:T(8,128)S(1)} %get-tuple-element.65, f32[64,256,64]{1,2,0:T(8,128)} %copy-done.2), kind=kOutput, calls=%fused_computation.89 | convolution fusion | flops 273682688 | bytes 13647872 | tf_op jit(solution)/shard_map/while/body/eval_jaxpr/qij,qid->qjd/dot_general | solution.py:50
  698.0 26.2 %scatter_fusion.1 = f32[64,64,128]{2,1,0:T(8,128)S(1)} fusion(f32[64,64,128]{2,1,0:T(8,128)S(1)} %broadcast.50.clone.1, s32[256]{0:T(256)S(1)} %bitcast.313, f32[256,64,128]{2,1,0:T(8,128)} %bitcast.254), kind=kCustom, calls=%fused_computation.3 | custom fusion | flops 2097152 | bytes 25166848 | tf_op jit(solution)/shard_map/while/body/eval_jaxpr/scatter-add | solution.py:62
  724.4 16.7 %copy.109 = bf16[1,4096,128]{2,0,1:T(2,128)(2,1)S(1)} copy(bf16[1,4096,128]{2,1,0:T(8,128)(2,1)S(1)} %bitcast.264) | data formatting | bytes 2097152 | tf_op jit(solution)/shard_map/reshape;transpose;reshape | solution.py:84
  741.1 22.4 %reduce.6 = bf16[4096,128]{1,0:T(8,128)(2,1)S(1)} reduce(bf16[4096,1,128]{2,1,0:T(2,128)(2,1)S(1)} %bitcast.256, bf16[]{:T(256)} %broadcast.81), dimensions={1}, to_apply=%bitcast.237.reduce_sub_computation | reduce | bytes 2097154
  764.7 9.9 %all-to-all-start.7 = ((bf16[32,2,8192]{2,1,0:T(2,128)(2,1)}), bf16[32,2,8192]{2,1,0:T(2,128)(2,1)}, u32[]{:S(2)}, u32[]{:S(2)}) async-start(bf16[32,2,8192]{2,1,0:T(2,128)(2,1)} %reshape.159), calls=%async_computation.8 | async-start | bytes 2097152 | tf_op jit(solution)/shard_map/all_to_all | solution.py:120
  774.5 4.3 reshape.156
  779.7 1.3 copy.93
  781.0 4.3 reshape.158
  786.1 1.3 copy.94
  787.4 17.7 %all-to-all-done.7 = bf16[32,2,8192]{2,1,0:T(2,128)(2,1)} async-done(((bf16[32,2,8192]{2,1,0:T(2,128)(2,1)}), bf16[32,2,8192]{2,1,0:T(2,128)(2,1)}, u32[]{:S(2)}, u32[]{:S(2)}) %all-to-all-start.7) | async-done | bytes 1048608 | tf_op jit(solution)/shard_map/all_to_all | solution.py:120
  805.1 4.4 reshape.160
  810.6 1.6 copy.91
  812.2 1.3 copy.95
  813.5 1.6 convert_element_type.51
  (76 shorter events, 9.6 us)
Async XLA Ops:
  7.2 1.2 copy-start
  7.2 218.3 %reduce-scatter.3.cloned.1.call-start = ((), (), s32[]{:S(2)}) async-start(), calls=%async_computation.10 | async-start | bytes 9437184 | tf_op jit(solution)/shard_map/reduce_scatter | solution.py:87
  48.4 42.2 %all-to-all-start.2 = ((bf16[32,2,8192]{2,1,0:T(2,128)(2,1)}), bf16[32,2,8192]{2,1,0:T(2,128)(2,1)}, u32[]{:S(2)}, u32[]{:S(2)}) async-start(bf16[32,2,8192]{2,1,0:T(2,128)(2,1)} %reshape.147), calls=%async_computation.2 | async-start | bytes 2097152 | tf_op jit(solution)/shard_map/all_to_all | solution.py:72
  90.6 40.5 %all-to-all-start = ((bf16[32,2,8192]{2,1,0:T(2,128)(2,1)}), bf16[32,2,8192]{2,1,0:T(2,128)(2,1)}, u32[]{:S(2)}, u32[]{:S(2)}) async-start(bf16[32,2,8192]{2,1,0:T(2,128)(2,1)} %reshape.149), calls=%async_computation | async-start | bytes 2097152 | tf_op jit(solution)/shard_map/all_to_all | solution.py:71
  131.1 125.0 %all-to-all-start.1 = ((bf16[32,2,8192]{2,1,0:T(2,128)(2,1)}), bf16[32,2,8192]{2,1,0:T(2,128)(2,1)}, u32[]{:S(2)}, u32[]{:S(2)}) async-start(bf16[32,2,8192]{2,1,0:T(2,128)(2,1)} %reshape.151), calls=%async_computation.1 | async-start | bytes 2097152 | tf_op jit(solution)/shard_map/all_to_all | solution.py:70
  230.5 35.4 %copy-start.5 = (s32[64,4]{0,1:T(4,128)S(1)}, s32[64,4]{0,1:T(4,128)}, u32[]{:S(2)}) copy-start(s32[64,4]{0,1:T(4,128)} %param.11) | copy-start | bytes 3076
  256.1 48.9 %all-to-all-start.4 = ((bf16[32,2,8192]{2,1,0:T(2,128)(2,1)}), bf16[32,2,8192]{2,1,0:T(2,128)(2,1)}, u32[]{:S(2)}, u32[]{:S(2)}) async-start(bf16[32,2,8192]{2,1,0:T(2,128)(2,1)} %reshape.153), calls=%async_computation.5 | async-start | bytes 2097152 | tf_op jit(solution)/shard_map/all_to_all | solution.py:95
  265.9 268.8 %all-gather.2.cloned.1.call-start = ((), (), s32[]{:S(2)}) async-start(), calls=%async_computation.11 | async-start | bytes 9437184 | tf_op jit(solution)/shard_map/all_gather | solution.py:122
  300.2 2.0 copy-start.2
  327.0 41.6 %copy-start.3 = (bf16[1,32,128,128]{3,2,1,0:T(8,128)(2,1)S(1)}, bf16[1,32,128,128]{3,2,1,0:T(8,128)(2,1)}, u32[]{:S(2)}) copy-start(bf16[1,32,128,128]{3,2,1,0:T(8,128)(2,1)} %copy.84) | copy-start | bytes 3145732
  368.6 445.0 %reduce-scatter.5.cloned.1.call-start = ((), (), s32[]{:S(2)}) async-start(), calls=%async_computation.12 | async-start | bytes 4325376 | tf_op jit(solution)/shard_map/reduce_scatter | solution.py:123
  589.7 83.5 %all-to-all-start.5 = ((bf16[32,2,8192]{2,1,0:T(2,128)(2,1)}), bf16[32,2,8192]{2,1,0:T(2,128)(2,1)}, u32[]{:S(2)}, u32[]{:S(2)}) async-start(bf16[32,2,8192]{2,1,0:T(2,128)(2,1)} %reshape.155), calls=%async_computation.6 | async-start | bytes 2097152 | tf_op jit(solution)/shard_map/all_to_all | solution.py:118
  672.1 11.4 %copy-start.4 = (bf16[1,32,128,128]{3,2,1,0:T(8,128)(2,1)S(1)}, bf16[1,32,128,128]{3,2,1,0:T(8,128)(2,1)}, u32[]{:S(2)}) copy-start(bf16[1,32,128,128]{3,2,1,0:T(8,128)(2,1)} %copy.84) | copy-start | bytes 3145732
  673.2 91.4 %all-to-all-start.6 = ((bf16[32,2,8192]{2,1,0:T(2,128)(2,1)}), bf16[32,2,8192]{2,1,0:T(2,128)(2,1)}, u32[]{:S(2)}, u32[]{:S(2)}) async-start(bf16[32,2,8192]{2,1,0:T(2,128)(2,1)} %reshape.157), calls=%async_computation.7 | async-start | bytes 2097152 | tf_op jit(solution)/shard_map/all_to_all | solution.py:119
  764.7 40.4 %all-to-all-start.7 = ((bf16[32,2,8192]{2,1,0:T(2,128)(2,1)}), bf16[32,2,8192]{2,1,0:T(2,128)(2,1)}, u32[]{:S(2)}, u32[]{:S(2)}) async-start(bf16[32,2,8192]{2,1,0:T(2,128)(2,1)} %reshape.159), calls=%async_computation.8 | async-start | bytes 2097152 | tf_op jit(solution)/shard_map/all_to_all | solution.py:120
  805.1 10.1 %copy-start.1 = (bf16[8,128,512]{2,1,0:T(8,128)(2,1)S(1)}, bf16[8,128,512]{2,1,0:T(8,128)(2,1)}, u32[]{:S(2)}) copy-start(bf16[8,128,512]{2,1,0:T(8,128)(2,1)} %param.9) | copy-start | bytes 3145732
Sparse Core Ops, SparseCore 0:
  17.5 208.0 reduce-scatter.2
  368.7 165.9 all-gather.1
  544.5 137.2 reduce-scatter.4
